TPU v7x, 512 devices: a whole 4x4x16 slice. The times are simulated.
512 devices in a mesh: seq: 64 (over z, y), head: 8 (over x, core).
Axes of the slice: x: 4, y: 4, z: 16, core: 2. Of those that a mesh axis runs over, the one named last changes fastest.
Arguments:
- stream_x: bfloat16 [16384, 3072], P('seq', 'head')
- qkv_weight: bfloat16 [3072, 4608], P(None, 'head')
- short_lengths: int32 [32], replicated, may hold values from 1 to 256, 4096 in all
- cache_owner: int32 [16384, 1], P('seq'), may hold values from 0 to 63, as said below
Outputs:
- attended: bfloat16 [16384, 1536], P('seq', 'head')
- row_lse: float32 [16, 16384], P('head', 'seq')
- kv_cache: bfloat16 [32768, 3072], P('seq', 'head')
Inputs may be any that keep to these rules, and one draw needn't show every extreme that they name: `short_lengths`: the lengths sum to 4096 and the longest is exactly 256. `cache_owner`: the rows of one device form 256 / 8 aligned pages of 8 rows; all rows of a page name the same owner, and the pages of one device name different owners, so an owner takes either none or exactly 8 rows of one device.
All inputs are finite; a program needn't handle non-finite values.
Results may differ from a plain program's by a relative error of at most 0.0083.
Values may be sent and summed in bfloat16 or wider, within the bound.
No kernel may reach another device: no remote copies, remote signals or barrier semaphores. Data moves between devices by JAX's collectives and lax.ppermute only.
A program may use at most 128 MiB of HBM per device.

v0:
```python
import math
import jax
import jax.numpy as jnp
from jax import lax
from jax.sharding import PartitionSpec as P

HD = 96
neg_large = -1e30
rope_base = 10000.0


def boundaries(short_lengths, long_length):
    running = jnp.cumsum(short_lengths)
    return jnp.concatenate([jnp.zeros((1,), jnp.int32), running]) + long_length


def locate(row_ids, bounds):
    passed = row_ids[:, None] >= bounds[None, :]
    segment = jnp.sum(passed.astype(jnp.int32), axis=1)
    seg_begin = jnp.max(jnp.where(passed, bounds[None, :], 0), axis=1)
    return (segment, seg_begin)


def rotate(parts, position, head_dim):
    half_dim = head_dim // 2
    inverse_freq = rope_base ** (-jnp.arange(half_dim, dtype=jnp.float32) / half_dim)
    angle = position[:, None, None] * inverse_freq[None, None, :]
    cosine = jnp.cos(angle)
    sine_part = jnp.sin(angle)
    first_half = parts[..., :half_dim]
    second_half = parts[..., half_dim:]
    return jnp.concatenate(
        [
            first_half * cosine - second_half * sine_part,
            second_half * cosine + first_half * sine_part,
        ],
        axis=-1,
    )


def body(stream_x, qkv_weight, short_lengths, cache_owner):
    seq_count = lax.axis_size("seq")
    tok_count = stream_x.shape[0]
    heads_here = qkv_weight.shape[1] // (3 * HD)
    long_length = tok_count * (seq_count * 11 // 16)
    bounds = boundaries(short_lengths, long_length)
    pad_segment = short_lengths.shape[0] + 1
    first_row = lax.axis_index("seq") * tok_count
    row_ids = first_row + jnp.arange(tok_count, dtype=jnp.int32)
    segment, seg_begin = locate(row_ids, bounds)
    position = (row_ids - seg_begin).astype(jnp.float32)
    is_padding = segment == pad_segment
    projected = jnp.dot(
        lax.all_gather(stream_x, "head", axis=1, tiled=True),
        qkv_weight,
        preferred_element_type=jnp.float32,
    )
    projected = projected.reshape(tok_count, heads_here, 3, HD)
    queries = rotate(projected[:, :, 0], position, HD).astype(jnp.bfloat16)
    rotated_keys = rotate(projected[:, :, 1], position, HD).astype(jnp.bfloat16)
    values = projected[:, :, 2].astype(jnp.bfloat16)
    packed = jnp.stack([rotated_keys, values], axis=2).reshape(tok_count, heads_here * 2 * HD)
    score_scale = 1.0 / math.sqrt(HD)
    shard_piece = lax.all_gather(packed, "seq", axis=0, tiled=True)
    key_count = shard_piece.shape[0]
    key_ids = jnp.arange(key_count, dtype=jnp.int32)
    row_max = jnp.full((heads_here, tok_count), neg_large, jnp.float32)
    key_segment, unused = locate(key_ids, bounds)
    key_value = shard_piece.reshape(key_count, heads_here, 2, HD)
    scores = (
        jnp.einsum("qhe,khe->hqk", queries, key_value[:, :, 0], preferred_element_type=jnp.float32)
        * score_scale
    )
    allowed = (
        (key_segment[None, :] == segment[:, None])
        & (key_ids[None, :] <= row_ids[:, None])
        & (key_ids[None, :] >= 0)
    )
    new_max = jnp.maximum(row_max, jnp.max(jnp.where(allowed[None], scores, neg_large), axis=2))
    weights = jnp.where(allowed[None], jnp.exp(scores - new_max[:, :, None]), 0.0)
    denominator = jnp.sum(weights, axis=2)
    context = jnp.einsum(
        "hqk,khe->hqe",
        weights.astype(jnp.bfloat16),
        key_value[:, :, 1],
        preferred_element_type=jnp.float32,
    )
    running = (new_max, denominator, context)
    row_max, denominator, context = running
    context = context / denominator[:, :, None]
    row_lse = jnp.where(is_padding[None, :], 0.0, row_max + jnp.log(denominator))
    context = jnp.where(is_padding[None, :, None], 0.0, context)
    attended = (
        jnp.transpose(context, (1, 0, 2)).reshape(tok_count, heads_here * HD).astype(jnp.bfloat16)
    )
    capacity = 2 * tok_count // seq_count
    owner_ids = cache_owner[:, 0]
    one_hot = (owner_ids[:, None] == jnp.arange(seq_count, dtype=jnp.int32)[None, :]).astype(
        jnp.int32
    )
    owner_rank = jnp.sum(jnp.cumsum(one_hot, axis=0) * one_hot, axis=1) - 1
    slot_index = owner_ids * capacity + owner_rank
    cached = jnp.where(is_padding[:, None], jnp.zeros_like(packed), packed)
    outbox = (
        jnp.zeros((seq_count * capacity, packed.shape[1]), jnp.bfloat16).at[slot_index].set(cached)
    )
    received = lax.all_to_all(
        outbox.reshape(seq_count, capacity, packed.shape[1]),
        "seq",
        split_axis=0,
        concat_axis=0,
        tiled=True,
    )
    kv_cache = received.reshape(seq_count * capacity, packed.shape[1])
    return (attended, row_lse, kv_cache)


def solution(mesh):
    return jax.shard_map(
        body,
        mesh=mesh,
        in_specs=(P("seq", "head"), P(None, "head"), P(), P("seq", None)),
        out_specs=(P("seq", "head"), P("head", "seq"), P("seq", "head")),
        check_vma=False,
    )
```

profile of v0, /device:TPU:32, one launch (start us, length us, event | category | flops | bytes accessed | tf_op | source)
XLA Modules:
  0.0 311.0 jit_solution(13779810520924512798)
XLA Ops:
  7.2 0.0 all-gather.3.cloned.1.call-start
  7.2 0.7 all-gather.3.cloned.1.call-update
  7.9 0.0 all-gather.5.cloned.1.call-start
  8.0 1.6 copy.28
  9.6 0.8 reduce-window.18
  10.3 0.6 reduce
  11.0 0.7 add_add_fusion
  11.7 0.1 fusion.29
  11.8 0.4 copy-done.1
  12.2 0.9 multiply_cosine_fusion
  13.1 33.3 %all-gather.3.cloned.1.call-done = bf16[256,3072]{1,0:T(8,128)(2,1)} async-done(((bf16[256,384]{1,0:T(8,128)(2,1)}), bf16[256,3072]{1,0:T(8,128)(2,1)}) %all-gather.3.cloned.1.call-update) | async-done | bytes 1572880 | tf_op jit(solution)/shard_map/all_gather | solution.py:54
  46.5 2.5 fusion.35
  49.0 1.5 subtract_convert_fusion.1
  50.6 0.7 copy.32
  51.3 1.3 fusion.26
  52.6 2.0 reduce-window.19
  54.6 1.0 slice_reduce_fusion
  55.6 1.0 fusion.25
  56.6 1.7 convert_reduce_fusion
  58.3 0.7 compare_select_fusion.1
  59.0 1.6 broadcast_select_fusion
  60.7 1.7 copy.36
  62.4 2.6 scatter_custom_fusion
  65.0 15.8 %all-to-all-start = ((bf16[64,8,384]{2,1,0:T(8,128)(2,1)}), bf16[64,8,384]{2,1,0:T(8,128)(2,1)}, u32[]{:S(2)}, u32[]{:S(2)}) async-start(bf16[64,8,384]{2,1,0:T(8,128)(2,1)} %bitcast.67), calls=%async_computation | async-start | bytes 786432 | tf_op jit(solution)/shard_map/all_to_all | solution.py:107
  80.9 8.0 %fusion.4 = pred[256,16384]{1,0:T(8,128)(4,1)} fusion(s32[256]{0:T(256)S(1)} %iota_add_fusion, s32[16384]{0:T(1024)} %convert_reduce_fusion, s32[256]{0:T(256)S(1)} %get-tuple-element.3), kind=kLoop, calls=%fused_computation.7 | loop fusion | flops 12582912 | bytes 4261888 | tf_op jit(solution)/shard_map/and | solution.py:75
  88.9 21.2 %all-to-all-done = bf16[64,8,384]{2,1,0:T(8,128)(2,1)} async-done(((bf16[64,8,384]{2,1,0:T(8,128)(2,1)}), bf16[64,8,384]{2,1,0:T(8,128)(2,1)}, u32[]{:S(2)}, u32[]{:S(2)}) %all-to-all-start) | async-done | bytes 393248 | tf_op jit(solution)/shard_map/all_to_all | solution.py:107
  110.1 141.5 %all-gather.5.cloned.1.call-done = bf16[16384,384]{0,1:T(8,128)(2,1)} async-done(((bf16[256,384]{0,1:T(8,128)(2,1)}), bf16[16384,384]{0,1:T(8,128)(2,1)}) %all-gather.5.cloned.1.call-update) | async-done | bytes 12582928 | tf_op jit(solution)/shard_map/all_gather | solution.py:64
  251.6 17.4 %select_reduce_fusion = (f32[2,256]{1,0:T(2,128)S(1)}, f32[2,256,16384]{2,1,0:T(8,128)}) fusion(pred[256,16384]{1,0:T(8,128)(4,1)} %fusion.4, bf16[16384,2,2,96]{0,3,2,1:T(8,128)(2,1)} %bitcast.76, bf16[256,2,48]{0,2,1:T(8,128)(2,1)} %get-tuple-element.8, bf16[256,2,48]{0,2,1:T(8,128)(2,1)} %get-tuple-element.7), kind=kOutput, calls=%fused_computation.2 | convolution fusion | flops 1635974656 | bytes 44140544 | tf_op jit(solution)/shard_map/qhe,khe->hqk/dot_general | solution.py:71
  269.0 15.9 %fusion = f32[2,256]{1,0:T(2,128)S(1)} fusion(f32[2,256,16384]{2,1,0:T(8,128)} %get-tuple-element.16, f32[2,256]{1,0:T(2,128)S(1)} %broadcast_maximum_fusion, pred[256,16384]{1,0:T(8,128)(4,1)} %fusion.4), kind=kLoop, calls=%fused_computation.3 | loop fusion | flops 33553920 | bytes 37752832 | tf_op jit(solution)/shard_map/reduce_sum | solution.py:81
  284.8 0.6 add_select_fusion
  285.4 16.9 %fusion.16 = bf16[256,2,96]{0,2,1:T(8,128)(2,1)} fusion(bf16[16384,2,2,96]{0,3,2,1:T(8,128)(2,1)} %bitcast.77, f32[2,256,16384]{2,1,0:T(8,128)} %get-tuple-element.16, f32[2,256]{1,0:T(2,128)S(1)} %broadcast_maximum_fusion, pred[256,16384]{1,0:T(8,128)(4,1)} %fusion.4, f32[256,2]{0,1:T(2,128)S(1)} %bitcast.72, pred[256]{0:T(512)(128)(4,1)S(1)} %broadcast_compare_fusion), kind=kOutput, calls=%fused_computation.17 | convolution fusion | flops 1644314624 | bytes 44142848 | tf_op jit(solution)/shard_map/hqk,khe->hqe/dot_general | solution.py:82
  302.4 1.8 copy.51
  (15 shorter events, 0.2 us)
Async XLA Ops:
  7.2 39.3 %copy-start = (bf16[3072,576]{0,1:T(8,128)(2,1)S(1)}, bf16[3072,576]{0,1:T(8,128)(2,1)}, u32[]{:S(2)}) copy-start(bf16[3072,576]{0,1:T(8,128)(2,1)} %param.5) | copy-start | bytes 10616836
  7.2 39.3 %all-gather.3.cloned.1.call-start = ((), (), s32[]{:S(2)}) async-start(), calls=%async_computation.1 | async-start | bytes 1769472 | tf_op jit(solution)/shard_map/all_gather | solution.py:54
  7.9 243.7 %all-gather.5.cloned.1.call-start = ((), (), s32[]{:S(2)}) async-start(), calls=%async_computation.2 | async-start | bytes 12779520 | tf_op jit(solution)/shard_map/all_gather | solution.py:64
  11.7 0.5 copy-start.1
  65.0 45.1 %all-to-all-start = ((bf16[64,8,384]{2,1,0:T(8,128)(2,1)}), bf16[64,8,384]{2,1,0:T(8,128)(2,1)}, u32[]{:S(2)}, u32[]{:S(2)}) async-start(bf16[64,8,384]{2,1,0:T(8,128)(2,1)} %bitcast.67), calls=%async_computation | async-start | bytes 786432 | tf_op jit(solution)/shard_map/all_to_all | solution.py:107
Sparse Core Ops, SparseCore 0:
  10.1 36.2 all-gather.2
  51.4 200.1 all-gather.4
where the time goes:
time: 312 us; the launch traced here: 311 us
  waiting for transfers between devices  197 us (63%)
  other arithmetic  37.5 us (12%)
  matrix products  36.8 us (12%)
  starting transfers between devices  15.9 us (5%)
  between operations  14.1 us (5%)
  local copies, waits for them, and re-layouts  9.93 us (3%)
    all_gather x1, waiting for transfers between devices, body(): shard_piece = lax.all_gather(packed, 'seq', axis=0, tiled=True)  142 us
    all_gather x1, waiting for transfers between devices, body(): lax.all_gather(stream_x, 'head', axis=1, tiled=True)  33.3 us
    all_to_all x1, waiting for transfers between devices, body(): lax.all_to_all(outbox.reshape(seq_count, capacity, packed.shape[1]), 'seq...  21.2 us
    dot_general x1, matrix products, body(): jnp.einsum('qhe,khe->hqk', queries, key_value[:, :, 0], preferred_element...  17.4 us
    dot_general x1, matrix products, body(): jnp.einsum('hqk,khe->hqe', weights.astype(jnp.bfloat16), key_value[:, :,...  16.9 us
    reduce_sum x1, other arithmetic, body(): denominator = jnp.sum(weights, axis=2)  15.9 us
    all_to_all x1, starting transfers between devices, body(): lax.all_to_all(outbox.reshape(seq_count, capacity, packed.shape[1]), 'seq...  15.8 us
    and x1, other arithmetic, body(): (key_segment[None, :] == segment[:, None]) & (key_ids[None, :] <= row_ids...  8.02 us
  transfers between devices with their start and end apart: 3, of which 3 were waited for; matrix products, arithmetic and copies ran while one was open for 9% of the time, Pallas kernels for 0%

commit v1 on v0

--- a/solution.py
+++ b/solution.py
@@ -1,3 +1,4 @@
+import functools
 import math
 import jax
 import jax.numpy as jnp
@@ -7,6 +8,15 @@
 HD = 96
 neg_large = -1e30
 rope_base = 10000.0
+
+
+def post_the_joints(z_in, join_dim):
+    return jnp.concatenate(
+        lax.all_to_all(jnp.stack(lax.axis_size("seq") * [z_in], 0), "seq", 0, 0), join_dim
+    )
+
+
+process_numbers_over_axis = functools.partial(post_the_joints, join_dim=0)
 
 
 def boundaries(short_lengths, long_length):
@@ -61,7 +71,7 @@
     values = projected[:, :, 2].astype(jnp.bfloat16)
     packed = jnp.stack([rotated_keys, values], axis=2).reshape(tok_count, heads_here * 2 * HD)
     score_scale = 1.0 / math.sqrt(HD)
-    shard_piece = lax.all_gather(packed, "seq", axis=0, tiled=True)
+    shard_piece = process_numbers_over_axis(packed)
     key_count = shard_piece.shape[0]
     key_ids = jnp.arange(key_count, dtype=jnp.int32)
     row_max = jnp.full((heads_here, tok_count), neg_large, jnp.float32)

time: 312 us -> 751 us (2.41)
  the two profiles are of different devices: /device:TPU:32 before, /device:TPU:8 now
where the time goes in v1:
time: 751 us; the launch traced here: 750 us
  waiting for transfers between devices  569 us (76%)
  local copies, waits for them, and re-layouts  44.9 us (6%)
  blocking collectives  43.1 us (6%)
  matrix products  38.8 us (5%)
  other arithmetic  33.7 us (4%)
  between operations  14.2 us (2%)
    all_to_all x1, waiting for transfers between devices, post_the_joints(): lax.all_to_all(jnp.stack(lax.axis_size('seq') * [z_in], 0), 'seq', 0, 0)  541 us
    all_to_all x1, blocking collectives, body(): lax.all_to_all(outbox.reshape(seq_count, capacity, packed.shape[1]), 'seq...  43.1 us
    all_gather x1, waiting for transfers between devices, body(): lax.all_gather(stream_x, 'head', axis=1, tiled=True)  27.4 us
    another operation x1, local copies, waits for them, and re-layouts, body(): key_value = shard_piece.reshape(key_count, heads_here, 2, HD)  19.5 us
    dot_general x1, matrix products, body(): jnp.einsum('qhe,khe->hqk', queries, key_value[:, :, 0], preferred_element...  18.5 us
    dot_general x1, matrix products, body(): jnp.einsum('hqk,khe->hqe', weights.astype(jnp.bfloat16), key_value[:, :,...  17.8 us
    reduce_sum x1, other arithmetic, body(): denominator = jnp.sum(weights, axis=2)  15.9 us
  transfers between devices with their start and end apart: 2, of which 2 were waited for; matrix products, arithmetic and copies ran while one was open for 3% of the time, Pallas kernels for 0%

profile of v1, /device:TPU:8, one launch (start us, length us, event | category | flops | bytes accessed | tf_op | source)
XLA Modules:
  0.0 750.1 jit_solution(1783660177433897865)
XLA Ops:
  7.2 0.0 copy-start
  7.2 0.0 all-gather.2.cloned.1.call-start
  7.2 0.7 all-gather.2.cloned.1.call-update
  7.9 1.7 copy.38
  9.6 0.8 reduce-window.18
  10.3 0.6 reduce
  11.0 1.3 fusion.26
  12.3 2.0 reduce-window.19
  14.3 1.0 slice_reduce_fusion
  15.3 0.7 add_add_fusion
  16.1 0.1 fusion.29
  16.2 0.9 fusion.25
  17.2 1.2 compare_select_fusion.1
  18.4 0.9 multiply_cosine_fusion
  19.3 27.4 %all-gather.2.cloned.1.call-done = bf16[256,3072]{1,0:T(8,128)(2,1)} async-done(((bf16[256,384]{1,0:T(8,128)(2,1)}), bf16[256,3072]{1,0:T(8,128)(2,1)}) %all-gather.2.cloned.1.call-update) | async-done | bytes 1572880 | tf_op jit(solution)/shard_map/all_gather | solution.py:64
  46.7 2.5 fusion.35
  49.3 0.9 subtract_convert_fusion.1
  50.3 0.2 copy.47
  50.5 1.7 scatter_custom_fusion
  52.2 43.1 %all_to_all.10 = bf16[64,8,384]{2,1,0:T(8,128)(2,1)} all-to-all(bf16[64,8,384]{2,1,0:T(8,128)(2,1)S(1)} %bitcast.69), channel_id=1, replica_groups=mesh['seq'=64,'head'=8] {'seq'}, dimensions={0} | all-to-all | bytes 786432 | tf_op jit(solution)/shard_map/all_to_all | solution.py:117
  95.3 6.0 stack.9
  101.3 6.1 all-to-all-start
  107.5 0.5 convert_reduce_fusion
  107.9 7.2 fusion.4
  115.1 541.2 %all-to-all-done = bf16[64,256,384]{1,2,0:T(8,128)(2,1)} async-done(((bf16[64,256,384]{1,2,0:T(8,128)(2,1)}), bf16[64,256,384]{1,2,0:T(8,128)(2,1)}, u32[]{:S(2)}, u32[]{:S(2)}) %all-to-all-start) | async-done | bytes 12582944 | tf_op jit(solution)/shard_map/all_to_all | solution.py:15
  656.3 14.0 %copy.43 = bf16[64,256,384]{1,0,2:T(8,128)(2,1)} copy(bf16[64,256,384]{1,2,0:T(8,128)(2,1)} %all-to-all-done) | data formatting | bytes 25165824 | tf_op jit(solution)/shard_map/all_to_all | solution.py:15
  670.3 19.5 %reshape_reshape.3 = bf16[16384,2,2,96]{0,3,2,1:T(8,128)(2,1)} reshape(bf16[64,256,384]{1,0,2:T(8,128)(2,1)} %copy.43) | data formatting | bytes 25165824 | tf_op jit(solution)/shard_map/reshape;reshape | solution.py:79
  689.8 18.5 %select_reduce_fusion = (f32[2,256]{1,0:T(2,128)S(1)}, f32[2,256,16384]{2,1,0:T(8,128)}) fusion(pred[256,16384]{1,0:T(8,128)(4,1)} %fusion.4, bf16[16384,2,2,96]{0,3,2,1:T(8,128)(2,1)} %reshape_reshape.3, bf16[256,2,48]{0,2,1:T(8,128)(2,1)S(1)} %get-tuple-element.8, bf16[256,2,48]{0,2,1:T(8,128)(2,1)S(1)} %get-tuple-element.7), kind=kOutput, calls=%fused_computation.2 | convolution fusion | flops 1635974656 | bytes 44140544 | tf_op jit(solution)/shard_map/qhe,khe->hqk/dot_general | solution.py:81
  708.3 15.9 %fusion = f32[2,256]{1,0:T(2,128)S(1)} fusion(f32[2,256,16384]{2,1,0:T(8,128)} %get-tuple-element.16, f32[2,256]{1,0:T(2,128)S(1)} %broadcast_maximum_fusion, pred[256,16384]{1,0:T(8,128)(4,1)} %fusion.4), kind=kLoop, calls=%fused_computation.3 | loop fusion | flops 33553920 | bytes 37752832 | tf_op jit(solution)/shard_map/reduce_sum | solution.py:91
  724.2 0.6 add_select_fusion
  724.8 17.8 %fusion.16 = bf16[256,2,96]{0,2,1:T(8,128)(2,1)} fusion(bf16[16384,2,2,96]{0,3,2,1:T(8,128)(2,1)} %reshape_reshape.3, f32[2,256,16384]{2,1,0:T(8,128)} %get-tuple-element.16, f32[2,256]{1,0:T(2,128)S(1)} %broadcast_maximum_fusion, pred[256,16384]{1,0:T(8,128)(4,1)} %fusion.4, f32[256,2]{0,1:T(2,128)S(1)} %bitcast.74, ...), kind=kOutput, calls=%fused_computation.17 | convolution fusion | flops 1644314624 | bytes 44142848 | tf_op jit(solution)/shard_map/hqk,khe->hqe/dot_general | solution.py:92
  742.5 0.7 copy.62
  (18 shorter events, 0.2 us)
Async XLA Ops:
  7.2 39.6 %copy-start = (bf16[3072,576]{0,1:T(8,128)(2,1)S(1)}, bf16[3072,576]{0,1:T(8,128)(2,1)}, u32[]{:S(2)}) copy-start(bf16[3072,576]{0,1:T(8,128)(2,1)} %param.5) | copy-start | bytes 10616836
  7.2 39.5 %all-gather.2.cloned.1.call-start = ((), (), s32[]{:S(2)}) async-start(), calls=%async_computation.2 | async-start | bytes 1769472 | tf_op jit(solution)/shard_map/all_gather | solution.py:64
  101.3 555.0 %all-to-all-start = ((bf16[64,256,384]{1,2,0:T(8,128)(2,1)}), bf16[64,256,384]{1,2,0:T(8,128)(2,1)}, u32[]{:S(2)}, u32[]{:S(2)}) async-start(bf16[64,256,384]{1,2,0:T(8,128)(2,1)} %stack.9), calls=%async_computation | async-start | bytes 25165824 | tf_op jit(solution)/shard_map/all_to_all | solution.py:15
  724.8 17.8 %copy-start.2 = (bf16[64,8,384]{2,1,0:T(8,128)(2,1)S(1)}, bf16[64,8,384]{2,1,0:T(8,128)(2,1)}, u32[]{:S(2)}) copy-start(bf16[64,8,384]{2,1,0:T(8,128)(2,1)} %all_to_all.10) | copy-start | bytes 1179652
  724.8 18.5 %copy-start.1 = (bf16[3072,576]{0,1:T(8,128)(2,1)S(1)}, bf16[3072,576]{0,1:T(8,128)(2,1)}, u32[]{:S(2)}) copy-start(bf16[3072,576]{0,1:T(8,128)(2,1)} %param.5) | copy-start | bytes 10616836
Sparse Core Ops, SparseCore 0:
  10.1 36.5 all-gather.1
